TPU v7x, 32 devices: a whole 2x2x4 slice. The times are simulated.
32 devices in a mesh: rep: 8 (over z, x), tp: 4 (over y, core).
Axes of the slice: x: 2, y: 2, z: 4, core: 2. Of those that a mesh axis runs over, the one named last changes fastest.
Arguments:
- hidden: bfloat16 [8192, 14336], P('rep', 'tp'), may hold values from -6 to 6
- grad_out: bfloat16 [8192, 2048], P('rep'), may hold values from -6 to 6
- weight: bfloat16 [8, 14336, 2048], P('rep', 'tp'), may hold values from -0.125 to 0.125
- alive: int32 [8, 4], replicated, may hold values from 0 to 1, as said below
Outputs:
- grad_hidden: bfloat16 [8192, 14336], P('rep', 'tp')
- grad_weight: float32 [7168, 2048], P('tp', 'rep')
Inputs may be any that keep to these rules, and one draw needn't show every extreme that they name: `alive`: exactly 2 replicas have exactly two zeros in their row; every other row is all ones.
All inputs are finite; a program needn't handle non-finite values.
Results may differ from a plain program's by a relative error of at most 0.001.
Values may be sent and summed in bfloat16 or wider, within the bound.
A program may use at most 128 MiB of HBM per device.

v0:
```python
import jax
import jax.numpy as jnp
from jax import lax
from jax.sharding import PartitionSpec as P

FF = 7168


def from_behind(x, axis, by):
    size = lax.axis_size(axis)
    pairs = [(i, i + by) for i in range(size) if 0 <= i + by < size]
    return lax.ppermute(x, axis, pairs)


def local(hidden, grad_out, weight, alive):
    replica = lax.axis_index("rep")
    tensor_index = lax.axis_index("tp")
    tensor_count = lax.axis_size("tp")
    replica_count = lax.axis_size("rep")
    slot_width = hidden.shape[1]
    common_width = FF // tensor_count
    alive_row = lax.dynamic_slice_in_dim(alive, replica, 1, 0)[0]
    live_count = jnp.sum(alive_row)
    slice_width = FF // live_count
    live_rank = jnp.cumsum(alive_row) - alive_row
    self_alive = alive_row[tensor_index]
    product = lax.dot_general(
        grad_out, weight[0], (((1,), (1,)), ((), ())), preferred_element_type=jnp.float32
    )
    columns = jnp.arange(slot_width)
    usable = (columns < slice_width) & (self_alive == 1)
    grad_hidden = jnp.where(usable[None, :], product, 0.0).astype(jnp.bfloat16)

    def common_part(source_block, source_dev, receiver):
        present = (source_dev >= 0) & (source_dev < tensor_count)
        holder = jnp.clip(source_dev, 0, tensor_count - 1)
        offset_cols = common_width * receiver - live_rank[holder] * slice_width
        live_src = (alive_row[holder] == 1) & present
        padded = jnp.pad(source_block, ((0, 0), (slot_width, slot_width)))
        first_col = jnp.clip(offset_cols + slot_width, 0, 2 * slot_width)
        window = lax.dynamic_slice_in_dim(padded, first_col, common_width, 1)
        position = jnp.arange(common_width) + offset_cols
        wanted = (position >= 0) & (position < slice_width) & live_src
        return jnp.where(wanted[None, :], window, jnp.zeros((), jnp.bfloat16))

    common = common_part(hidden, tensor_index, tensor_index)
    for offset in (-2, -1, 1, 2):
        piece = common_part(hidden, tensor_index, tensor_index - offset)
        common = common + from_behind(piece, "tp", -offset)
    factor = float(replica_count * grad_out.shape[0]) ** (-0.5)
    partial_value = lax.dot_general(
        common, grad_out, (((0,), (0,)), ((), ())), preferred_element_type=jnp.float32
    )
    owned_sum = lax.psum_scatter(partial_value, "rep", scatter_dimension=1, tiled=True)
    return (grad_hidden, owned_sum * factor)


def solution(mesh):
    return jax.shard_map(
        local,
        mesh=mesh,
        in_specs=(P("rep", "tp"), P("rep", None), P("rep", "tp", None), P()),
        out_specs=(P("rep", "tp"), P("tp", "rep")),
        check_vma=False,
    )
```

profile of v0, /device:TPU:21, one launch (start us, length us, event | category | flops | bytes accessed | tf_op | source)
XLA Modules:
  0.0 425.0 jit_solution(9838277275169547940)
XLA Ops:
  7.2 0.0 reduce-scatter.2.cloned.1.call-start
  7.2 1.4 dynamic-slice_reduce_fusion
  10.6 0.2 reduce-window.9
  10.8 0.6 dynamic_slice.37
  12.0 1.4 fusion.40
  14.1 12.6 %fusion.11 = (bf16[1024,1792]{1,0:T(8,128)(2,1)}, bf16[1024,1792]{1,0:T(8,128)(2,1)}, bf16[1024,1792]{1,0:T(8,128)(2,1)}, bf16[1024,1792]{1,0:T(8,128)(2,1)}) fusion(s32[]{:T(128)S(6)} %min.28, bf16[1024,3584]{1,0:T(8,128)(2,1)} %param.4, pred[1792]{0:T(1024)(128)(4,1)S(1)} %get-tuple-element.10, s32[]{:T(128)S(6)} %min.29, ...), kind=kLoop, calls=%fused_computation.14 | loop fusion | flops 7340032 | bytes 22027280 | tf_op jit(solution)/shard_map/jit(_where)/select_n | solution.py:44
  26.8 1.3 collective-permute-start
  28.1 1.3 collective-permute-start.1
  29.4 5.1 %collective-permute-start.2 = (bf16[1024,1792]{1,0:T(8,128)(2,1)}, bf16[1024,1792]{1,0:T(8,128)(2,1)}, u32[]{:S(2)}, u32[]{:S(2)}) collective-permute-start(bf16[1024,1792]{1,0:T(8,128)(2,1)} %get-tuple-element.6), channel_id=1, source_target_pairs={{1,0},{2,1},{3,2},{5,4},{6,5},{7,6},{9,8},{10,9},{11,10},{13,12},{... | collective-permute-start | bytes 11010056 | tf_op jit(solution)/shard_map/ppermute | solution.py:12
  34.4 7.4 %collective-permute-start.3 = (bf16[1024,1792]{1,0:T(8,128)(2,1)}, bf16[1024,1792]{1,0:T(8,128)(2,1)}, u32[]{:S(2)}, u32[]{:S(2)}) collective-permute-start(bf16[1024,1792]{1,0:T(8,128)(2,1)} %get-tuple-element.7), channel_id=1, source_target_pairs={{2,0},{3,1},{6,4},{7,5},{10,8},{11,9},{14,12},{15,13},{18,16},{19,... | collective-permute-start | bytes 11010056 | tf_op jit(solution)/shard_map/ppermute | solution.py:12
  41.8 67.4 %collective-permute-done = bf16[1024,1792]{1,0:T(8,128)(2,1)} collective-permute-done((bf16[1024,1792]{1,0:T(8,128)(2,1)}, bf16[1024,1792]{1,0:T(8,128)(2,1)}, u32[]{:S(2)}, u32[]{:S(2)}) %collective-permute-start) | collective-permute-done | bytes 3670048 | tf_op jit(solution)/shard_map/ppermute | solution.py:12
  109.2 0.0 collective-permute-done.1
  109.2 0.0 collective-permute-done.2
  109.2 10.3 %collective-permute-done.3 = bf16[1024,1792]{1,0:T(8,128)(2,1)} collective-permute-done((bf16[1024,1792]{1,0:T(8,128)(2,1)}, bf16[1024,1792]{1,0:T(8,128)(2,1)}, u32[]{:S(2)}, u32[]{:S(2)}) %collective-permute-start.3) | collective-permute-done | bytes 3670048 | tf_op jit(solution)/shard_map/ppermute | solution.py:12
  119.5 22.1 %fusion.9 = f32[1792,2048]{1,0:T(8,128)} fusion(bf16[1024,2048]{1,0:T(8,128)(2,1)} %param.5, bf16[1024,1792]{1,0:T(8,128)(2,1)} %collective-permute-done.3, bf16[1024,1792]{1,0:T(8,128)(2,1)} %collective-permute-done.2, bf16[1024,1792]{1,0:T(8,128)(2,1)} %collective-permute-done.1, bf16[1024,1792]{1,0:T(8,128)(2,1)} %collective-permute-done, s32[]{:T(128)S(6)} %min.27, ...), kind=kOutput, calls=%fused_computation.13 | convolution fusion | flops 7536377856 | bytes 40896260 | tf_op jit(solution)/shard_map/dot_general | solution.py:51
  141.6 0.0 reduce-scatter.2.cloned.1.call-update
  142.2 21.7 %select_convert_fusion = bf16[1024,3584]{1,0:T(8,128)(2,1)} fusion(bf16[1024,2048]{1,0:T(8,128)(2,1)} %param.5, bf16[1,3584,2048]{2,1,0:T(8,128)(2,1)} %param.6, pred[3584]{0:T(1024)(128)(4,1)S(1)} %fusion.17), kind=kOutput, calls=%fused_computation.7 | convolution fusion | flops 15039725568 | bytes 26217984 | tf_op jit(solution)/shard_map/dot_general | solution.py:27
  163.9 251.4 %reduce-scatter.2.cloned.1.call-done = f32[1792,256]{1,0:T(8,128)} async-done(((f32[1792,2048]{1,0:T(8,128)}), f32[1792,256]{1,0:T(8,128)}) %reduce-scatter.2.cloned.1.call-update) | async-done | bytes 1835024 | tf_op jit(solution)/shard_map/reduce_scatter | solution.py:54
  415.3 2.9 broadcast_multiply_fusion
  (5 shorter events, 0.0 us)
Async XLA Ops:
  7.2 408.1 %reduce-scatter.2.cloned.1.call-start = ((), (), s32[]{:S(2)}) async-start(), calls=%async_computation.1 | async-start | bytes 16515072 | tf_op jit(solution)/shard_map/reduce_scatter | solution.py:54
  26.8 82.4 %collective-permute-start = (bf16[1024,1792]{1,0:T(8,128)(2,1)}, bf16[1024,1792]{1,0:T(8,128)(2,1)}, u32[]{:S(2)}, u32[]{:S(2)}) collective-permute-start(bf16[1024,1792]{1,0:T(8,128)(2,1)} %get-tuple-element.4), channel_id=1, source_target_pairs={{0,2},{1,3},{4,6},{5,7},{8,10},{9,11},{12,14},{13,15},{16,18},{17,... | collective-permute-start | bytes 11010056 | tf_op jit(solution)/shard_map/ppermute | solution.py:12
  28.1 81.1 %collective-permute-start.1 = (bf16[1024,1792]{1,0:T(8,128)(2,1)}, bf16[1024,1792]{1,0:T(8,128)(2,1)}, u32[]{:S(2)}, u32[]{:S(2)}) collective-permute-start(bf16[1024,1792]{1,0:T(8,128)(2,1)} %get-tuple-element.5), channel_id=1, source_target_pairs={{0,1},{1,2},{2,3},{4,5},{5,6},{6,7},{8,9},{9,10},{10,11},{12,13},{... | collective-permute-start | bytes 11010056 | tf_op jit(solution)/shard_map/ppermute | solution.py:12
  29.4 79.8 %collective-permute-start.2 = (bf16[1024,1792]{1,0:T(8,128)(2,1)}, bf16[1024,1792]{1,0:T(8,128)(2,1)}, u32[]{:S(2)}, u32[]{:S(2)}) collective-permute-start(bf16[1024,1792]{1,0:T(8,128)(2,1)} %get-tuple-element.6), channel_id=1, source_target_pairs={{1,0},{2,1},{3,2},{5,4},{6,5},{7,6},{9,8},{10,9},{11,10},{13,12},{... | collective-permute-start | bytes 11010056 | tf_op jit(solution)/shard_map/ppermute | solution.py:12
  34.4 85.1 %collective-permute-start.3 = (bf16[1024,1792]{1,0:T(8,128)(2,1)}, bf16[1024,1792]{1,0:T(8,128)(2,1)}, u32[]{:S(2)}, u32[]{:S(2)}) collective-permute-start(bf16[1024,1792]{1,0:T(8,128)(2,1)} %get-tuple-element.7), channel_id=1, source_target_pairs={{2,0},{3,1},{6,4},{7,5},{10,8},{11,9},{14,12},{15,13},{18,16},{19,... | collective-permute-start | bytes 11010056 | tf_op jit(solution)/shard_map/ppermute | solution.py:12
Sparse Core Ops, SparseCore 0:
  141.7 273.5 reduce-scatter.1
where the time goes:
time: 428 us; the launch traced here: 425 us
  waiting for transfers between devices  329 us (77%)
  matrix products  43.8 us (10%)
  between operations  18 us (4%)
  other arithmetic  17.2 us (4%)
  starting transfers between devices  15.1 us (4%)
    reduce_scatter x1, waiting for transfers between devices, local(): lax.psum_scatter(partial_value, 'rep', scatter_dimension=1, tiled=True)  251 us
    ppermute x4, waiting for transfers between devices, from_behind(): return lax.ppermute(x, axis, pairs)  77.6 us
    dot_general x1, matrix products, local(): lax.dot_general(common, grad_out, (((0,), (0,)), ((), ())), preferred_ele...  22.1 us
    dot_general x1, matrix products, local(): lax.dot_general(grad_out, weight[0], (((1,), (1,)), ((), ())), preferred_...  21.7 us
    ppermute x4, starting transfers between devices, from_behind(): return lax.ppermute(x, axis, pairs)  15 us
    select_n x1, other arithmetic, common_part(): return jnp.where(wanted[None, :], window, jnp.zeros((), jnp.bfloat16))  12.6 us
  transfers between devices with their start and end apart: 5, of which 3 were waited for; matrix products, arithmetic and copies ran while one was open for 5% of the time, Pallas kernels for 0%

commit v1 on v0

v1 whole, which is shorter than its diff:
```python
import itertools

import jax
import jax.numpy as jnp
from jax import lax
from jax.sharding import PartitionSpec as P

FF = 7168
LANES = 128
CHUNKS = 3
TOP = 60000.0


def possible_edges(count):
    common = FF // count
    edges = set()
    rows = [[1] * count]
    for lost in itertools.combinations(range(count), 2):
        rows.append([int(i not in lost) for i in range(count)])
    for row in rows:
        if not sum(row):
            continue
        width = FF // sum(row)
        rank = 0
        for i in range(count):
            if row[i]:
                low, high = rank * width, (rank + 1) * width
                for j in range(count):
                    if low < (j + 1) * common and j * common < high:
                        edges.add((i, j))
                rank += 1
    return edges


def rep_masks(count):
    masks, bit = [], 1
    while bit < count:
        masks.append(bit)
        bit *= 2
    if len(masks) >= 3:
        masks[2] |= masks[1]
    return masks


def swap(x, axis, mask):
    size = lax.axis_size(axis)
    return lax.ppermute(x, axis, [(i, i ^ mask) for i in range(size)])


def chunk_bounds(width, parts):
    unit = LANES if width % LANES == 0 else width // 7
    units = width // unit
    parts = min(parts, units)
    cuts = [units * k // parts * unit for k in range(parts + 1)]
    return list(zip(cuts[:-1], cuts[1:]))


def local(hidden, grad_out, weight, alive):
    replica = lax.axis_index("rep")
    tensor_index = lax.axis_index("tp")
    tensor_count = lax.axis_size("tp")
    replica_count = lax.axis_size("rep")
    slot_width = hidden.shape[1]
    common_width = FF // tensor_count
    features = grad_out.shape[1]
    owned = features // replica_count
    alive_row = lax.dynamic_slice_in_dim(alive, replica, 1, 0)[0]
    live_count = jnp.sum(alive_row)
    slice_width = FF // live_count
    live_rank = jnp.cumsum(alive_row) - alive_row
    self_alive = alive_row[tensor_index]
    self_rank = live_rank[tensor_index]
    edges = possible_edges(tensor_count)
    masks = rep_masks(replica_count)

    most = jnp.stack([jnp.max(jnp.abs(hidden)), jnp.max(jnp.abs(grad_out))]).astype(jnp.float32)
    most = jnp.broadcast_to(most[:, None], (2, LANES))
    for axis, list_of in (("tp", rep_masks(tensor_count)), ("rep", masks)):
        for mask in list_of:
            most = jnp.maximum(most, swap(most, axis, mask))
    tokens = float(replica_count * grad_out.shape[0])
    bound = jnp.maximum(most[0, 0] * most[1, 0], 1e-30) * tokens
    scale = TOP / bound

    padded = jnp.pad(hidden, ((0, 0), (slot_width, slot_width)))

    def part_for(receiver, low, high):
        offset_cols = common_width * receiver - self_rank * slice_width + low
        first_col = jnp.clip(offset_cols + slot_width, 0, 2 * slot_width)
        window = lax.dynamic_slice_in_dim(padded, first_col, high - low, 1)
        position = jnp.arange(high - low) + offset_cols
        wanted = (position >= 0) & (position < slice_width) & (self_alive == 1)
        return jnp.where(wanted[None, :], window, jnp.zeros((), jnp.bfloat16))

    def relative(order):
        blocks = []
        for place in range(replica_count):
            owner = replica
            for level, i in enumerate(order):
                if place >> (len(order) - 1 - level) & 1:
                    owner = owner ^ masks[i]
            blocks.append(lax.dynamic_slice_in_dim(grad_out, owner * owned, owned, 1))
        return jnp.concatenate(blocks, 1)

    levels = len(masks)
    orders = [[(k + i) % levels for i in range(levels)] for k in range(levels)]
    bounds = chunk_bounds(common_width, CHUNKS)
    ordered = {}
    for k in range(len(bounds)):
        if k % levels not in ordered:
            ordered[k % levels] = relative(orders[k % levels])

    commons = []
    for low, high in bounds:
        common = part_for(tensor_index, low, high)
        for offset in (-2, -1, 1, 2):
            pairs = [(i, i + offset) for i in range(tensor_count) if (i, i + offset) in edges]
            if pairs:
                common = common + lax.ppermute(part_for(tensor_index + offset, low, high), "tp", pairs)
        commons.append(common)

    def contract(common, other):
        return lax.dot_general(
            common, other, (((0,), (0,)), ((), ())), preferred_element_type=jnp.float32
        ) * scale

    sums = []
    for k, common in enumerate(commons):
        other = ordered[k % levels]
        half = features // 2
        sent = contract(common, other[:, half:]).astype(jnp.float16)
        kept = contract(common, other[:, :half])
        for level, i in enumerate(orders[k % levels]):
            kept = kept + swap(sent, "rep", masks[i]).astype(jnp.float32)
            half = kept.shape[1] // 2
            if level < levels - 1:
                sent = kept[:, half:].astype(jnp.float16)
                kept = kept[:, :half]
        sums.append(kept)

    product = lax.dot_general(
        grad_out, weight[0], (((1,), (1,)), ((), ())), preferred_element_type=jnp.float32
    )
    columns = jnp.arange(slot_width)
    usable = (columns < slice_width) & (self_alive == 1)
    grad_hidden = jnp.where(usable[None, :], product, 0.0).astype(jnp.bfloat16)
    return (grad_hidden, jnp.concatenate(sums, 0) * (bound * (tokens**-0.5 / TOP)))


def solution(mesh):
    return jax.shard_map(
        local,
        mesh=mesh,
        in_specs=(P("rep", "tp"), P("rep", None), P("rep", "tp", None), P()),
        out_specs=(P("rep", "tp"), P("tp", "rep")),
        check_vma=False,
    )
```

time: 428 us -> 250 us (0.58)
  waiting for transfers between devices: 329 us -> 130 us
  starting transfers between devices: 15.1 us -> 38.3 us
  other arithmetic: 17.2 us -> 34.5 us
  matrix products: 43.8 us -> 31.4 us
  between operations: 18 us -> 5.9 us
  local copies, waits for them, and re-layouts: 1.97 us -> 9.61 us
    reduce_scatter x1 -> x0, waiting for transfers between devices: 251 us -> none  [local(): lax.psum_scatter(partial_value, 'rep', scatter_dimension=1, tiled=True)]
    ppermute x4 -> x26, waiting for transfers between devices: 77.6 us -> 130 us  [the longest x14 102 us: swap(): return lax.ppermute(x, axis, [(i, i ^ mask) for i in range(size)])]
    ppermute x4 -> x26, starting transfers between devices: 15 us -> 38.3 us  [the longest x12 25 us: local(): lax.ppermute(part_for(tensor_index + offset, low, high), 'tp', pairs)]
    add x0 -> x11, other arithmetic: none -> 11.4 us  [the longest x2 8.98 us: local(): common + lax.ppermute(part_for(tensor_index + offset, low, high), 'tp', p...]
    dot_general x1 -> x6, matrix products: 22.1 us -> 10.9 us  [contract(): lax.dot_general(common, other, (((0,), (0,)), ((), ())), preferred_elemen...]
    dynamic_slice x2 -> x3, local copies, waits for them, and re-layouts: 1.97 us -> 6.67 us  [the longest x1 4.81 us: relative(): blocks.append(lax.dynamic_slice_in_dim(grad_out, owner * owned, owned, 1))]
    select_n x1 -> x3, other arithmetic: 12.6 us -> 14.9 us  [part_for(): return jnp.where(wanted[None, :], window, jnp.zeros((), jnp.bfloat16))]
  transfers between devices with their start and end apart: 5 -> 26, of which waited for: 3 -> 12; matrix products, arithmetic and copies ran while one was open for 5% -> 25% of each run, Pallas kernels for 0% -> 0%
where the time goes in v1:
time: 250 us
  waiting for transfers between devices  130 us (52%)
  starting transfers between devices  38.3 us (15%)
  other arithmetic  34.5 us (14%)
  matrix products  31.4 us (13%)
  local copies, waits for them, and re-layouts  9.61 us (4%)
  between operations  5.9 us (2%)
    ppermute x14, waiting for transfers between devices, swap(): return lax.ppermute(x, axis, [(i, i ^ mask) for i in range(size)])  102 us
    ppermute x12, waiting for transfers between devices, local(): lax.ppermute(part_for(tensor_index + offset, low, high), 'tp', pairs)  27.9 us
    ppermute x12, starting transfers between devices, local(): lax.ppermute(part_for(tensor_index + offset, low, high), 'tp', pairs)  25 us
    dot_general x1, matrix products, local(): lax.dot_general(grad_out, weight[0], (((1,), (1,)), ((), ())), preferred_...  20.5 us
    select_n x3, other arithmetic, part_for(): return jnp.where(wanted[None, :], window, jnp.zeros((), jnp.bfloat16))  14.9 us
    ppermute x14, starting transfers between devices, swap(): return lax.ppermute(x, axis, [(i, i ^ mask) for i in range(size)])  13.3 us
    dot_general x6, matrix products, contract(): lax.dot_general(common, other, (((0,), (0,)), ((), ())), preferred_elemen...  10.9 us
    add x2, other arithmetic, local(): common + lax.ppermute(part_for(tensor_index + offset, low, high), 'tp', p...  8.98 us
  transfers between devices with their start and end apart: 26, of which 12 were waited for; matrix products, arithmetic and copies ran while one was open for 25% of the time, Pallas kernels for 0%

profile of v1, /device:TPU:21, one launch (start us, length us, event | category | flops | bytes accessed | tf_op | source)
XLA Modules:
  0.0 249.7 jit_solution(8978832317337442826)
XLA Ops:
  7.5 5.8 %fusion.63 = (bf16[1024,512]{1,0:T(8,128)(2,1)}, bf16[1024,512]{1,0:T(8,128)(2,1)}, bf16[1024,512]{1,0:T(8,128)(2,1)}, bf16[1024,512]{1,0:T(8,128)(2,1)}) fusion(s32[]{:T(128)S(6)} %min.47, bf16[1024,3584]{1,0:T(8,128)(2,1)} %param.4, pred[512]{0:T(512)(128)(4,1)S(1)} %get-tuple-element.41, s32[]{:T(128)S(6)} %min.48, ...), kind=kLoop, calls=%fused_computation.89 | loop fusion | flops 2097152 | bytes 11536400 | tf_op jit(solution)/shard_map/jit(_where)/select_n | solution.py:93
  14.0 5.3 %collective-permute-start.1 = (bf16[1024,512]{1,0:T(8,128)(2,1)}, bf16[1024,512]{1,0:T(8,128)(2,1)}, u32[]{:S(2)}, u32[]{:S(2)}) collective-permute-start(bf16[1024,512]{1,0:T(8,128)(2,1)} %get-tuple-element.5), channel_id=1, source_target_pairs={{1,0},{2,1},{3,2},{5,4},{6,5},{7,6},{9,8},{10,9},{11,10},{13,12},{... | collective-permute-start | bytes 3145736 | tf_op jit(solution)/shard_map/ppermute | solution.py:119
  20.6 1.6 collective-permute-start.3
  22.2 1.6 abs_reduce_fusion
  23.8 1.4 abs_reduce_fusion.1
  28.9 2.1 collective-permute-start.5
  31.0 14.4 %collective-permute-done.5 = f32[2,128]{1,0:T(2,128)S(1)} collective-permute-done((f32[2,128]{1,0:T(2,128)S(1)}, f32[2,128]{1,0:T(2,128)S(1)}, u32[]{:S(2)}, u32[]{:S(2)}) %collective-permute-start.5) | collective-permute-done | bytes 1056 | tf_op jit(solution)/shard_map/ppermute | solution.py:47
  49.1 7.8 %fusion.55 = (bf16[1024,640]{1,0:T(8,128)(2,1)}, bf16[1024,640]{1,0:T(8,128)(2,1)}, bf16[1024,640]{1,0:T(8,128)(2,1)}, bf16[1024,640]{1,0:T(8,128)(2,1)}, bf16[1...) fusion(s32[]{:T(128)S(6)} %min.52, bf16[1024,3584]{1,0:T(8,128)(2,1)} %param.4, ...), kind=kLoop, calls=%fused_computation.78 | loop fusion | flops 3932160 | bytes 15208216 | tf_op jit(solution)/shard_map/jit(_where)/select_n | solution.py:93
  57.1 2.4 collective-permute-done.8
  59.5 1.7 collective-permute-start.12
  61.2 3.8 %collective-permute-start.13 = (bf16[1024,640]{1,0:T(8,128)(2,1)}, bf16[1024,640]{1,0:T(8,128)(2,1)}, u32[]{:S(2)}, u32[]{:S(2)}) collective-permute-start(bf16[1024,640]{1,0:T(8,128)(2,1)} %get-tuple-element.11), channel_id=1, source_target_pairs={{1,0},{2,1},{3,2},{5,4},{6,5},{7,6},{9,8},{10,9},{11,10},{13,12},{... | collective-permute-start | bytes 3932168 | tf_op jit(solution)/shard_map/ppermute | solution.py:119
  65.0 1.5 collective-permute-start.14
  66.5 20.5 %select_convert_fusion = bf16[1024,3584]{1,0:T(8,128)(2,1)} fusion(bf16[1024,2048]{1,0:T(8,128)(2,1)S(1)} %copy-done.2, bf16[1,3584,2048]{2,1,0:T(8,128)(2,1)} %param.6, pred[3584]{0:T(1024)(128)(4,1)S(1)} %fusion.67), kind=kOutput, calls=%fused_computation.17 | convolution fusion | flops 15039725568 | bytes 26217984 | tf_op jit(solution)/shard_map/dot_general | solution.py:141
  87.1 4.8 %constant_dynamic-slice_fusion.7 = (bf16[1024,256]{1,0:T(8,128)(2,1)S(1)}, bf16[1024,256]{1,0:T(8,128)(2,1)}, bf16[1024,256]{1,0:T(8,128)(2,1)}, bf16[1024,256]{...) fusion(bf16[1024,2048]{1,0:T(8,128)(2,1)} %param.5, ...), kind=kLoop, calls=%fused_computation.108 | loop fusion | bytes 13631540 | tf_op jit(solution)/shard_map/dynamic_slice | solution.py:102
  92.0 2.2 slice-done.1
  97.6 4.2 %collective-permute-start.20 = (bf16[1024,640]{1,0:T(8,128)(2,1)S(1)}, bf16[1024,640]{1,0:T(8,128)(2,1)}, u32[]{:S(2)}, u32[]{:S(2)}) collective-permute-start(bf16[1024,640]{1,0:T(8,128)(2,1)S(1)} %get-tuple-element.15), channel_id=1, source_target_pairs={{1,0},{2,1},{3,2},{5,4},{6,5},{7,6},{9,8},{10,9},{11,10},{13,12},{... | collective-permute-start | bytes 3932168 | tf_op jit(solution)/shard_map/ppermute | solution.py:119
  103.2 1.5 collective-permute-start.22
  106.5 3.0 %add_add_fusion.2 = bf16[1024,512]{1,0:T(8,128)(2,1)S(1)} fusion(bf16[1024,512]{1,0:T(8,128)(2,1)} %collective-permute-done.3, bf16[1024,512]{1,0:T(8,128)(2,1)} %collective-permute-done.2, bf16[1024,512]{1,0:T(8,128)(2,1)} %collective-permute-done.1, bf16[1024,512]{1,0:T(8,128)(2,1)S(1)} %collective-permute-done, s32[]{:T(128)S(6)} %min.46, ...), kind=kLoop, calls=%fused_computation.88 | loop fusion | flops 5767168 | bytes 12583428 | tf_op jit(solution)/shard_map/add | solution.py:119
  110.8 2.2 multiply_convert_fusion.2
  115.2 27.1 %collective-permute-done.22 = bf16[1024,640]{1,0:T(8,128)(2,1)} collective-permute-done((bf16[1024,640]{1,0:T(8,128)(2,1)S(1)}, bf16[1024,640]{1,0:T(8,128)(2,1)}, u32[]{:S(2)}, u32[]{:S(2)}) %collective-permute-start.22) | collective-permute-done | bytes 1310752 | tf_op jit(solution)/shard_map/ppermute | solution.py:119
  142.3 6.0 %add_add_fusion.1 = (bf16[1024,640]{1,0:T(8,128)(2,1)S(1)}, bf16[1024,640]{1,0:T(8,128)(2,1)S(1)}) fusion(bf16[1024,640]{1,0:T(8,128)(2,1)S(1)} %collective-permute-done.15, bf16[1024,640]{1,0:T(8,128)(2,1)} %collective-permute-done.14, bf16[1024,640]{1,0:T(8,128)(2,1)} %collective-permute-done.13, bf16[1024,640]{1,0:T(8,128)(2,1)} %collective-permute-done.12, ...), kind=kLoop, calls=%fused_computation.77 | loop fusion | flops 14417920 | bytes 20448520 | tf_op jit(solution)/shard_map/add | solution.py:119
  148.3 2.8 %multiply_convert_fusion.1 = f16[640,1024]{1,0:T(8,128)(2,1)S(1)} fusion(bf16[1024,640]{1,0:T(8,128)(2,1)S(1)} %get-tuple-element.8, bf16[1024,256]{1,0:T(8,128)(2,1)S(1)} %copy-done.18, bf16[1024,256]{1,0:T(8,128)(2,1)} %copy-done.20, bf16[1024,256]{1,0:T(8,128)(2,1)S(1)} %copy-done.19, bf16[1024,256]{1,0:T(8,128)(2,1)S(1)} %copy-done.10, f32[]{:T(128)} %bitcast.6), kind=kOutput, calls=%fused_computation.26 | convolution fusion | flops 1351876608 | bytes 4718596 | tf_op jit(solution)/shard_map/dot_general | solution.py:123
  151.1 2.0 collective-permute-start.16
  153.1 1.6 multiply_convert_fusion
  154.7 1.6 fusion.10
  156.5 1.6 fusion.14
  159.6 51.0 %collective-permute-done.16 = f16[640,1024]{1,0:T(8,128)(2,1)S(1)} collective-permute-done((f16[640,1024]{1,0:T(8,128)(2,1)S(1)}, f16[640,1024]{1,0:T(8,128)(2,1)S(1)}, u32[]{:S(2)}, u32[]{:S(2)}) %collective-permute-start.16) | collective-permute-done | bytes 1310752 | tf_op jit(solution)/shard_map/ppermute | solution.py:47
  211.4 20.3 %collective-permute-done.23 = f16[640,1024]{1,0:T(8,128)(2,1)S(1)} collective-permute-done((f16[640,1024]{1,0:T(8,128)(2,1)S(1)}, f16[640,1024]{1,0:T(8,128)(2,1)S(1)}, u32[]{:S(2)}, u32[]{:S(2)}) %collective-permute-start.23) | collective-permute-done | bytes 1310752 | tf_op jit(solution)/shard_map/ppermute | solution.py:47
  234.0 4.7 %collective-permute-done.17 = f16[640,512]{1,0:T(8,128)(2,1)S(1)} collective-permute-done((f16[640,512]{1,0:T(8,128)(2,1)S(1)}, f16[640,512]{1,0:T(8,128)(2,1)S(1)}, u32[]{:S(2)}, u32[]{:S(2)}) %collective-permute-start.17) | collective-permute-done | bytes 655392 | tf_op jit(solution)/shard_map/ppermute | solution.py:47
  240.2 1.7 collective-permute-done.24
  242.4 3.0 %collective-permute-done.18 = f16[640,256]{1,0:T(8,128)(2,1)S(1)} collective-permute-done((f16[640,256]{1,0:T(8,128)(2,1)S(1)}, f16[640,256]{1,0:T(8,128)(2,1)S(1)}, u32[]{:S(2)}, u32[]{:S(2)}) %collective-permute-start.18) | collective-permute-done | bytes 327712 | tf_op jit(solution)/shard_map/ppermute | solution.py:47
  245.6 2.7 %collective-permute-done.25 = f16[640,256]{1,0:T(8,128)(2,1)S(1)} collective-permute-done((f16[640,256]{1,0:T(8,128)(2,1)S(1)}, f16[640,256]{1,0:T(8,128)(2,1)S(1)}, u32[]{:S(2)}, u32[]{:S(2)}) %collective-permute-start.25) | collective-permute-done | bytes 327712 | tf_op jit(solution)/shard_map/ppermute | solution.py:47
  (121 shorter events, 30.1 us)
Async XLA Ops:
  13.2 48.0 %collective-permute-start = (bf16[1024,512]{1,0:T(8,128)(2,1)}, bf16[1024,512]{1,0:T(8,128)(2,1)S(1)}, u32[]{:S(2)}, u32[]{:S(2)}) collective-permute-start(bf16[1024,512]{1,0:T(8,128)(2,1)} %get-tuple-element.4), channel_id=1, source_target_pairs={{2,0},{6,4},{10,8},{14,12},{18,16},{22,20},{26,24},{30,28}} | collective-permute-start | bytes 3145736 | tf_op jit(solution)/shard_map/ppermute | solution.py:119
  14.0 51.1 %collective-permute-start.1 = (bf16[1024,512]{1,0:T(8,128)(2,1)}, bf16[1024,512]{1,0:T(8,128)(2,1)}, u32[]{:S(2)}, u32[]{:S(2)}) collective-permute-start(bf16[1024,512]{1,0:T(8,128)(2,1)} %get-tuple-element.5), channel_id=1, source_target_pairs={{1,0},{2,1},{3,2},{5,4},{6,5},{7,6},{9,8},{10,9},{11,10},{13,12},{... | collective-permute-start | bytes 3145736 | tf_op jit(solution)/shard_map/ppermute | solution.py:119
  19.3 76.2 %collective-permute-start.2 = (bf16[1024,512]{1,0:T(8,128)(2,1)}, bf16[1024,512]{1,0:T(8,128)(2,1)}, u32[]{:S(2)}, u32[]{:S(2)}) collective-permute-start(bf16[1024,512]{1,0:T(8,128)(2,1)} %get-tuple-element.6), channel_id=1, source_target_pairs={{0,1},{1,2},{2,3},{4,5},{5,6},{6,7},{8,9},{9,10},{10,11},{12,13},{... | collective-permute-start | bytes 3145736 | tf_op jit(solution)/shard_map/ppermute | solution.py:119
  20.6 76.2 %collective-permute-start.3 = (bf16[1024,512]{1,0:T(8,128)(2,1)}, bf16[1024,512]{1,0:T(8,128)(2,1)}, u32[]{:S(2)}, u32[]{:S(2)}) collective-permute-start(bf16[1024,512]{1,0:T(8,128)(2,1)} %get-tuple-element.7), channel_id=1, source_target_pairs={{1,3},{5,7},{9,11},{13,15},{17,19},{21,23},{25,27},{29,31}} | collective-permute-start | bytes 3145736 | tf_op jit(solution)/shard_map/ppermute | solution.py:119
  26.6 2.2 collective-permute-start.4
  28.9 16.4 %collective-permute-start.5 = (f32[2,128]{1,0:T(2,128)S(1)}, f32[2,128]{1,0:T(2,128)S(1)}, u32[]{:S(2)}, u32[]{:S(2)}) collective-permute-start(f32[2,128]{1,0:T(2,128)S(1)} %broadcast_maximum_fusion), channel_id=1, source_target_pairs={{0,2},{1,3},{2,0},{3,1},{4,6},{5,7},{6,4},{7,5},{8,10},{9,11},{10,... | collective-permute-start | bytes 3080 | tf_op jit(solution)/shard_map/ppermute | solution.py:47
  45.4 2.4 collective-permute-start.6
  47.8 9.1 %collective-permute-start.7 = (f32[2,128]{1,0:T(2,128)S(1)}, f32[2,128]{1,0:T(2,128)S(1)}, u32[]{:S(2)}, u32[]{:S(2)}) collective-permute-start(f32[2,128]{1,0:T(2,128)S(1)} %max.72), channel_id=1, source_target_pairs={{0,8},{4,12},{8,0},{12,4},{16,24},{20,28},{24,16},{28,20},{1,9},{5... | collective-permute-start | bytes 3080 | tf_op jit(solution)/shard_map/ppermute | solution.py:47
  57.0 2.5 collective-permute-start.8
  59.5 38.1 %collective-permute-start.12 = (bf16[1024,640]{1,0:T(8,128)(2,1)}, bf16[1024,640]{1,0:T(8,128)(2,1)}, u32[]{:S(2)}, u32[]{:S(2)}) collective-permute-start(bf16[1024,640]{1,0:T(8,128)(2,1)} %get-tuple-element.10), channel_id=1, source_target_pairs={{2,0},{6,4},{10,8},{14,12},{18,16},{22,20},{26,24},{30,28}} | collective-permute-start | bytes 3932168 | tf_op jit(solution)/shard_map/ppermute | solution.py:119
  61.2 40.7 %collective-permute-start.13 = (bf16[1024,640]{1,0:T(8,128)(2,1)}, bf16[1024,640]{1,0:T(8,128)(2,1)}, u32[]{:S(2)}, u32[]{:S(2)}) collective-permute-start(bf16[1024,640]{1,0:T(8,128)(2,1)} %get-tuple-element.11), channel_id=1, source_target_pairs={{1,0},{2,1},{3,2},{5,4},{6,5},{7,6},{9,8},{10,9},{11,10},{13,12},{... | collective-permute-start | bytes 3932168 | tf_op jit(solution)/shard_map/ppermute | solution.py:119
  65.0 38.1 %collective-permute-start.14 = (bf16[1024,640]{1,0:T(8,128)(2,1)}, bf16[1024,640]{1,0:T(8,128)(2,1)}, u32[]{:S(2)}, u32[]{:S(2)}) collective-permute-start(bf16[1024,640]{1,0:T(8,128)(2,1)} %get-tuple-element.12), channel_id=1, source_target_pairs={{0,1},{1,2},{2,3},{4,5},{5,6},{6,7},{8,9},{9,10},{10,11},{12,13},{... | collective-permute-start | bytes 3932168 | tf_op jit(solution)/shard_map/ppermute | solution.py:119
  91.9 17.6 %copy-start.14 = (bf16[1024,256]{1,0:T(8,128)(2,1)}, bf16[1024,256]{1,0:T(8,128)(2,1)S(1)}, u32[]{:S(2)}) copy-start(bf16[1024,256]{1,0:T(8,128)(2,1)S(1)} %get-tuple-element.27) | copy-start | bytes 1572868
  91.9 18.9 %copy-start.5 = (bf16[1024,256]{1,0:T(8,128)(2,1)}, bf16[1024,256]{1,0:T(8,128)(2,1)S(1)}, u32[]{:S(2)}) copy-start(bf16[1024,256]{1,0:T(8,128)(2,1)S(1)} %get-tuple-element.23) | copy-start | bytes 1572868
  91.9 18.9 %copy-start.7 = (bf16[1024,256]{1,0:T(8,128)(2,1)}, bf16[1024,256]{1,0:T(8,128)(2,1)S(1)}, u32[]{:S(2)}) copy-start(bf16[1024,256]{1,0:T(8,128)(2,1)S(1)} %get-tuple-element.24) | copy-start | bytes 1572868
  95.5 18.4 %collective-permute-start.15 = (bf16[1024,640]{1,0:T(8,128)(2,1)S(1)}, bf16[1024,640]{1,0:T(8,128)(2,1)S(1)}, u32[]{:S(2)}, u32[]{:S(2)}) collective-permute-start(bf16[1024,640]{1,0:T(8,128)(2,1)S(1)} %copy-done.4), channel_id=1, source_target_pairs={{1,3},{5,7},{9,11},{13,15},{17,19},{21,23},{25,27},{29,31}} | collective-permute-start | bytes 3932168 | tf_op jit(solution)/shard_map/ppermute | solution.py:119
  96.9 18.3 %collective-permute-start.19 = (bf16[1024,640]{1,0:T(8,128)(2,1)S(1)}, bf16[1024,640]{1,0:T(8,128)(2,1)S(1)}, u32[]{:S(2)}, u32[]{:S(2)}) collective-permute-start(bf16[1024,640]{1,0:T(8,128)(2,1)S(1)} %copy-done.3), channel_id=1, source_target_pairs={{2,0},{6,4},{10,8},{14,12},{18,16},{22,20},{26,24},{30,28}} | collective-permute-start | bytes 3932168 | tf_op jit(solution)/shard_map/ppermute | solution.py:119
  97.6 17.5 %collective-permute-start.20 = (bf16[1024,640]{1,0:T(8,128)(2,1)S(1)}, bf16[1024,640]{1,0:T(8,128)(2,1)}, u32[]{:S(2)}, u32[]{:S(2)}) collective-permute-start(bf16[1024,640]{1,0:T(8,128)(2,1)S(1)} %get-tuple-element.15), channel_id=1, source_target_pairs={{1,0},{2,1},{3,2},{5,4},{6,5},{7,6},{9,8},{10,9},{11,10},{13,12},{... | collective-permute-start | bytes 3932168 | tf_op jit(solution)/shard_map/ppermute | solution.py:119
  101.9 13.3 %collective-permute-start.21 = (bf16[1024,640]{1,0:T(8,128)(2,1)S(1)}, bf16[1024,640]{1,0:T(8,128)(2,1)}, u32[]{:S(2)}, u32[]{:S(2)}) collective-permute-start(bf16[1024,640]{1,0:T(8,128)(2,1)S(1)} %get-tuple-element.16), channel_id=1, source_target_pairs={{0,1},{1,2},{2,3},{4,5},{5,6},{6,7},{8,9},{9,10},{10,11},{12,13},{... | collective-permute-start | bytes 3932168 | tf_op jit(solution)/shard_map/ppermute | solution.py:119
  103.2 39.1 %collective-permute-start.22 = (bf16[1024,640]{1,0:T(8,128)(2,1)S(1)}, bf16[1024,640]{1,0:T(8,128)(2,1)}, u32[]{:S(2)}, u32[]{:S(2)}) collective-permute-start(bf16[1024,640]{1,0:T(8,128)(2,1)S(1)} %get-tuple-element.17), channel_id=1, source_target_pairs={{1,3},{5,7},{9,11},{13,15},{17,19},{21,23},{25,27},{29,31}} | collective-permute-start | bytes 3932168 | tf_op jit(solution)/shard_map/ppermute | solution.py:119
  113.1 35.2 %copy-start.10 = (bf16[1024,256]{1,0:T(8,128)(2,1)S(1)}, bf16[1024,256]{1,0:T(8,128)(2,1)}, u32[]{:S(2)}) copy-start(bf16[1024,256]{1,0:T(8,128)(2,1)} %copy-done.9) | copy-start | bytes 1572868
  113.1 35.2 %copy-start.18 = (bf16[1024,256]{1,0:T(8,128)(2,1)S(1)}, bf16[1024,256]{1,0:T(8,128)(2,1)}, u32[]{:S(2)}) copy-start(bf16[1024,256]{1,0:T(8,128)(2,1)} %get-tuple-element.19) | copy-start | bytes 1572868
  113.9 34.4 %copy-start.19 = (bf16[1024,256]{1,0:T(8,128)(2,1)S(1)}, bf16[1024,256]{1,0:T(8,128)(2,1)}, u32[]{:S(2)}) copy-start(bf16[1024,256]{1,0:T(8,128)(2,1)} %get-tuple-element.20) | copy-start | bytes 1572868
  113.9 44.2 %collective-permute-start.9 = (f16[512,1024]{1,0:T(8,128)(2,1)}, f16[512,1024]{1,0:T(8,128)(2,1)S(1)}, u32[]{:S(2)}, u32[]{:S(2)}) collective-permute-start(f16[512,1024]{1,0:T(8,128)(2,1)} %multiply_convert_fusion.2), channel_id=1, source_target_pairs={{0,4},{4,0},{8,12},{12,8},{16,20},{20,16},{24,28},{28,24},{1,5},{5... | collective-permute-start | bytes 3145736 | tf_op jit(solution)/shard_map/ppermute | solution.py:47
  151.1 59.5 %collective-permute-start.16 = (f16[640,1024]{1,0:T(8,128)(2,1)S(1)}, f16[640,1024]{1,0:T(8,128)(2,1)S(1)}, u32[]{:S(2)}, u32[]{:S(2)}) collective-permute-start(f16[640,1024]{1,0:T(8,128)(2,1)S(1)} %multiply_convert_fusion.1), channel_id=1, source_target_pairs={{0,8},{4,12},{8,0},{12,4},{16,24},{20,28},{24,16},{28,20},{1,9},{5... | collective-permute-start | bytes 3932168 | tf_op jit(solution)/shard_map/ppermute | solution.py:47
  156.3 75.3 %collective-permute-start.23 = (f16[640,1024]{1,0:T(8,128)(2,1)S(1)}, f16[640,1024]{1,0:T(8,128)(2,1)S(1)}, u32[]{:S(2)}, u32[]{:S(2)}) collective-permute-start(f16[640,1024]{1,0:T(8,128)(2,1)S(1)} %multiply_convert_fusion), channel_id=1, source_target_pairs={{0,24},{4,28},{8,16},{12,20},{16,8},{20,12},{24,0},{28,4},{1,25},{... | collective-permute-start | bytes 3932168 | tf_op jit(solution)/shard_map/ppermute | solution.py:47
  158.6 75.1 %collective-permute-start.10 = (f16[512,512]{1,0:T(8,128)(2,1)S(1)}, f16[512,512]{1,0:T(8,128)(2,1)S(1)}, u32[]{:S(2)}, u32[]{:S(2)}) collective-permute-start(f16[512,512]{1,0:T(8,128)(2,1)S(1)} %slice_convert_fusion.2), channel_id=1, source_target_pairs={{0,8},{4,12},{8,0},{12,4},{16,24},{20,28},{24,16},{28,20},{1,9},{5... | collective-permute-start | bytes 1572872 | tf_op jit(solution)/shard_map/ppermute | solution.py:47
  211.3 27.4 %collective-permute-start.17 = (f16[640,512]{1,0:T(8,128)(2,1)S(1)}, f16[640,512]{1,0:T(8,128)(2,1)S(1)}, u32[]{:S(2)}, u32[]{:S(2)}) collective-permute-start(f16[640,512]{1,0:T(8,128)(2,1)S(1)} %slice_convert_fusion.1), channel_id=1, source_target_pairs={{0,24},{4,28},{8,16},{12,20},{16,8},{20,12},{24,0},{28,4},{1,25},{... | collective-permute-start | bytes 1966088 | tf_op jit(solution)/shard_map/ppermute | solution.py:47
  232.4 9.5 %collective-permute-start.24 = (f16[640,512]{1,0:T(8,128)(2,1)S(1)}, f16[640,512]{1,0:T(8,128)(2,1)S(1)}, u32[]{:S(2)}, u32[]{:S(2)}) collective-permute-start(f16[640,512]{1,0:T(8,128)(2,1)S(1)} %slice_convert_fusion), channel_id=1, source_target_pairs={{0,4},{4,0},{8,12},{12,8},{16,20},{20,16},{24,28},{28,24},{1,5},{5... | collective-permute-start | bytes 1966088 | tf_op jit(solution)/shard_map/ppermute | solution.py:47
  233.9 8.4 %collective-permute-start.11 = (f16[512,256]{1,0:T(8,128)(2,1)S(1)}, f16[512,256]{1,0:T(8,128)(2,1)S(1)}, u32[]{:S(2)}, u32[]{:S(2)}) collective-permute-start(f16[512,256]{1,0:T(8,128)(2,1)S(1)} %slice_convert_fusion.5), channel_id=1, source_target_pairs={{0,24},{4,28},{8,16},{12,20},{16,8},{20,12},{24,0},{28,4},{1,25},{... | collective-permute-start | bytes 786440 | tf_op jit(solution)/shard_map/ppermute | solution.py:47
  239.0 6.5 %collective-permute-start.18 = (f16[640,256]{1,0:T(8,128)(2,1)S(1)}, f16[640,256]{1,0:T(8,128)(2,1)S(1)}, u32[]{:S(2)}, u32[]{:S(2)}) collective-permute-start(f16[640,256]{1,0:T(8,128)(2,1)S(1)} %slice_convert_fusion.4), channel_id=1, source_target_pairs={{0,4},{4,0},{8,12},{12,8},{16,20},{20,16},{24,28},{28,24},{1,5},{5... | collective-permute-start | bytes 983048 | tf_op jit(solution)/shard_map/ppermute | solution.py:47
  242.2 6.0 %collective-permute-start.25 = (f16[640,256]{1,0:T(8,128)(2,1)S(1)}, f16[640,256]{1,0:T(8,128)(2,1)S(1)}, u32[]{:S(2)}, u32[]{:S(2)}) collective-permute-start(f16[640,256]{1,0:T(8,128)(2,1)S(1)} %slice_convert_fusion.3), channel_id=1, source_target_pairs={{0,8},{4,12},{8,0},{12,4},{16,24},{20,28},{24,16},{28,20},{1,9},{5... | collective-permute-start | bytes 983048 | tf_op jit(solution)/shard_map/ppermute | solution.py:47
  (17 other events, 128.4 us)
